TPU v7x, 32 devices: a whole 2x2x4 slice. The times are simulated.
32 devices in a mesh: chan: 16 (over z, y, x), blk: 2 (over core).
Axes of the slice: x: 2, y: 2, z: 4, core: 2. Of those that a mesh axis runs over, the one named last changes fastest.
Arguments:
- generator: bfloat16 [16, 1536, 1536], P('chan', 'blk'), may hold values from -6 to 6
- hamiltonian: bfloat16 [16, 1536, 1536], P('chan', 'blk'), may hold values from -0.15625 to 0.15625
- pp_occupancy: float32 [16, 1536], P('chan'), may hold values from -1 to 1
- ph_occupancy: float32 [16, 1536], P('chan'), may hold values from -1 to 1
- lengths: int32 [16], P('chan'), may hold values from 384 to 1536, as said below
- partner: int32 [16, 16], P('chan'), may hold values from 0 to 15, each once within a row
- coupling: float32 [16, 16], P('chan'), may hold values from 0.5 to 2
- degeneracy: float32 [16], P('chan'), may hold values from 1 to 30
- orbital: int32 [16, 1536], P('chan', 'blk'), may hold values from 0 to 239
Outputs:
- two_body: bfloat16 [16, 1536, 1536], P('chan', 'blk')
- one_body: float32 [240], replicated
Inputs may be any that keep to these rules, and one draw needn't show every extreme that they name: `lengths`: some channel has the full length 1536.
All inputs are finite; a program needn't handle non-finite values.
Results may differ from a plain program's by a relative error of at most 0.007.
Values may be sent and summed in bfloat16 or wider, within the bound.
A program may use at most 128 MiB of HBM per device.

v0:
```python
import functools
import math

import jax
import jax.numpy as jnp
from jax import lax
from jax.experimental import pallas as pl
from jax.experimental.pallas import tpu as pltpu
from jax.sharding import PartitionSpec as P

NOB = 240
MESH = pl.DeviceIdType.MESH
VMEM_LIMIT = 60 * 1024 * 1024


def scaled_copy(matrix, occupancy):
    return (matrix.astype(jnp.float32) * occupancy[None, :]).astype(jnp.bfloat16)


def make_fold(left_scaled, right_scaled, pieces):
    return jnp.dot(left_scaled, pieces[1], preferred_element_type=jnp.float32) - jnp.dot(
        right_scaled, pieces[0], preferred_element_type=jnp.float32
    )


def on_device_plain(
    generator,
    hamiltonian,
    pp_occupancy,
    ph_occupancy,
    lengths,
    partner,
    coupling,
    degeneracy,
    orbital,
):
    chan_count = lax.axis_size("chan")
    blk_index = lax.axis_index("blk")
    row_count = generator.shape[1]
    columns = generator.shape[2]
    piece_rows = row_count // chan_count
    col_ids = jnp.arange(columns, dtype=jnp.int32)
    row_ids = blk_index * row_count + jnp.arange(row_count, dtype=jnp.int32)
    live_mask = (row_ids[:, None] < lengths[0]) & (col_ids[None, :] < lengths[0])
    nothing = jnp.zeros((), jnp.bfloat16)
    gen_live = jnp.where(live_mask, generator[0], nothing)
    ham_live = jnp.where(live_mask, hamiltonian[0], nothing)
    gen_scaled = scaled_copy(gen_live, pp_occupancy[0])
    ham_scaled = scaled_copy(ham_live, pp_occupancy[0])
    owner_ids = jnp.arange(chan_count, dtype=jnp.int32)
    matches = partner[0][None, :] == owner_ids[:, None]
    sender_slot = jnp.sum(jnp.where(matches, owner_ids[None, :], 0), axis=1)
    scales = coupling[0]
    scales_slot = scales[sender_slot]
    ph_occ = ph_occupancy[0]
    gen_send = (
        gen_live.reshape(chan_count, piece_rows, columns)[sender_slot].astype(jnp.float32)
        * scales_slot[:, None, None]
    ).astype(jnp.bfloat16)
    ham_send = (
        ham_live.reshape(chan_count, piece_rows, columns)[sender_slot].astype(jnp.float32)
        * scales_slot[:, None, None]
    ).astype(jnp.bfloat16)
    gen_recv, ham_recv = (
        lax.all_to_all(gen_send, "chan", split_axis=0, concat_axis=0, tiled=True),
        lax.all_to_all(ham_send, "chan", split_axis=0, concat_axis=0, tiled=True),
    )
    ladder = make_fold(
        gen_scaled,
        ham_scaled,
        (
            lax.all_gather(gen_live, "blk", axis=0, tiled=True),
            lax.all_gather(ham_live, "blk", axis=0, tiled=True),
        ),
    )
    gen_rows = gen_recv.reshape(row_count, columns)
    ham_rows = ham_recv.reshape(row_count, columns)
    crossed = make_fold(
        scaled_copy(gen_rows, ph_occ),
        scaled_copy(ham_rows, ph_occ),
        (
            lax.all_gather(gen_rows, "blk", axis=0, tiled=True),
            lax.all_gather(ham_rows, "blk", axis=0, tiled=True),
        ),
    )
    crossed_back = crossed.astype(jnp.bfloat16).reshape(chan_count, piece_rows, columns)
    returned = lax.all_to_all(crossed_back, "chan", split_axis=0, concat_axis=0, tiled=True)
    restored = (returned[partner[0]].astype(jnp.float32) * scales[:, None, None]).reshape(
        row_count, columns
    )
    combined = jnp.where(live_mask, ladder + restored, jnp.zeros((), jnp.float32))
    two_body = combined.astype(jnp.bfloat16)[None]
    own_block = lax.dynamic_slice_in_dim(combined, blk_index * row_count, row_count, 1)
    weighted = jnp.diagonal(own_block) * degeneracy[0]
    orbit_match = orbital[0][:, None] == jnp.arange(NOB, dtype=jnp.int32)[None, :]
    partial_sums = jnp.sum(jnp.where(orbit_match, weighted[:, None], 0.0), axis=0)
    normalizer = 8.0 * math.sqrt(chan_count * columns / NOB)
    one_body = lax.psum(partial_sums, ("chan", "blk")) / normalizer
    return (two_body, one_body)


def widths_of(columns):
    unit = 256
    inner = columns - 2 * unit
    if inner <= 0 or inner % (2 * unit):
        return (unit,) * (columns // unit)
    return (unit,) + (2 * unit,) * (inner // (2 * unit)) + (unit,)


def fused_kernel(n, m, widths, scale, *refs):
    parts = len(widths)
    (
        gen_hbm,
        ham_hbm,
        pp_ref,
        ph_ref,
        partner_ref,
        coupling_ref,
        length_ref,
        weight_ref,
        orbital_ref,
        out_hbm,
        sum_ref,
        own_g,
        own_h,
        far_g,
        far_h,
        send_g,
        send_h,
        cross_g,
        cross_h,
        left,
        right,
        lad,
        out,
        diag,
        part,
        slots,
    ) = refs[:26]
    back = refs[26 : 26 + parts]
    ret = refs[26 + parts : 26 + 2 * parts]
    (
        own_sem,
        x_send,
        x_recv,
        a_send,
        a_recv,
        r_send,
        r_recv,
        l_sem,
        b_send,
        b_recv,
        out_sem,
        t_send,
        t_recv,
    ) = refs[26 + 2 * parts :]
    c = lax.axis_index("chan")
    b = lax.axis_index("blk")
    ob = 1 - b
    me = c * m + b
    count = n * m
    piece, columns = gen_hbm.shape[1:]
    rows = n * piece
    orbits = part.shape[1]
    twin = (c, ob)
    starts = [sum(widths[:j]) for j in range(parts)]
    raw = ((gen_hbm, own_g, far_g), (ham_hbm, own_h, far_h))
    sent = ((send_g, cross_g), (send_h, cross_h))
    length = length_ref[0]

    def half_cols(half):
        return pl.ds(pl.multiple_of(half * rows, 128), rows)

    def slot(half, d):
        return pl.ds(pl.multiple_of((half * n + d) * piece, piece), piece)

    def strip(d):
        return pl.ds(pl.multiple_of(d * piece, piece), piece)

    def offset(i):
        q = i // 2
        turn = q % 2
        far = n // 2 + (1 - 2 * turn) * ((q + 1) // 2)
        near = (1 - turn) * (n - 1 - q // 2) + turn * ((q + 1) // 2)
        return (1 - i % 2) * far + (i % 2) * near

    def target(i):
        return (c + offset(i)) % n

    def source(i):
        return (c + n - offset(i)) % n

    def each(count, body, first=0):
        def step(i, carry):
            body(i)
            return carry

        lax.fori_loop(first, count, step, 0)

    def own_copy(t):
        return pltpu.make_async_copy(raw[t][0], raw[t][1], own_sem.at[t])

    def twin_copy(t):
        return pltpu.make_async_remote_copy(
            src_ref=raw[t][0],
            dst_ref=raw[t][2],
            send_sem=x_send.at[t],
            recv_sem=x_recv.at[t],
            device_id=twin,
            device_id_type=MESH,
        )

    def piece_copy(t, k, d):
        return pltpu.make_async_remote_copy(
            src_ref=sent[t][0].at[strip(k)],
            dst_ref=sent[t][1].at[slot(b, d)],
            send_sem=a_send.at[t, k],
            recv_sem=a_recv.at[t, d],
            device_id=(k, b),
            device_id_type=MESH,
        )

    def relay(t, half, d):
        return pltpu.make_async_remote_copy(
            src_ref=sent[t][1].at[slot(half, d)],
            dst_ref=sent[t][1].at[slot(half, d)],
            send_sem=r_send.at[t, d],
            recv_sem=r_recv.at[t, d],
            device_id=twin,
            device_id_type=MESH,
        )

    def back_copy(j, k, d):
        return pltpu.make_async_remote_copy(
            src_ref=back[j].at[strip(k)],
            dst_ref=ret[j].at[d],
            send_sem=b_send.at[j, k],
            recv_sem=b_recv.at[j, d],
            device_id=(k, b),
            device_id_type=MESH,
        )

    def back_local(j):
        return pltpu.make_async_copy(back[j].at[strip(c)], ret[j].at[c], l_sem.at[j])

    def out_copy(j):
        cols = pl.ds(starts[j], widths[j])
        return pltpu.make_async_copy(out.at[:, cols], out_hbm.at[:, cols], out_sem.at[j])

    def peer(i):
        return (me + 1 + i) % count

    def total_copy(to, origin):
        return pltpu.make_async_remote_copy(
            src_ref=part,
            dst_ref=slots.at[origin],
            send_sem=t_send.at[to],
            recv_sem=t_recv.at[origin],
            device_id=(to // m, to % m),
            device_id_type=MESH,
        )

    for t in range(2):
        own_copy(t).start()
    barrier = pltpu.get_barrier_semaphore()

    def greet(i):
        to = peer(i)
        pl.semaphore_signal(barrier, inc=1, device_id=(to // m, to % m), device_id_type=MESH)

    each(count - 1, greet)
    for t in range(2):
        own_copy(t).wait()

    col_live = lax.broadcasted_iota(jnp.int32, (1, columns), 1) < length
    row_ids = lax.broadcasted_iota(jnp.int32, (piece, 1), 0)

    def prepare(k, refs_at):
        p, weight = jnp.int32(0), jnp.float32(0.0)
        for q in range(n):
            match = partner_ref[q] == k
            p = jnp.where(match, q, p)
            weight = jnp.where(match, coupling_ref[q], weight)
        factor = jnp.where(col_live, weight, 0.0)
        factor = jnp.where(row_ids + (b * n + p) * piece < length, factor, 0.0)
        for t in range(2):
            dst, where = refs_at[t]
            dst[where, :] = (raw[t][1][p].astype(jnp.float32) * factor).astype(jnp.bfloat16)

    def prepare_sent(i):
        k = target(i)
        prepare(k, [(send_g, strip(k)), (send_h, strip(k))])

    def send(i):
        k = target(i)
        for t in range(2):
            piece_copy(t, k, c).start()

    prepare_sent(0)
    pl.semaphore_wait(barrier, count - 1)

    def prepare_and_send(i):
        prepare_sent(i)
        send(i - 1)

    each(n - 1, prepare_and_send, 1)
    prepare(c, [(cross_g, slot(b, c)), (cross_h, slot(b, c))])
    send(n - 2)
    for t in range(2):
        twin_copy(t).start()

    def pp_scale(i):
        factor = jnp.where(col_live, pp_ref[...], 0.0)
        left[strip(i), :] = (own_g[i].astype(jnp.float32) * factor).astype(jnp.bfloat16)
        right[strip(i), :] = (own_h[i].astype(jnp.float32) * factor).astype(jnp.bfloat16)

    each(n, pp_scale)

    def dot(x, y):
        return jnp.dot(x, y, preferred_element_type=jnp.float32)

    for t in range(2):
        relay(t, b, c).start()
        twin_copy(t).wait_recv()
    unit = 256

    def ladder_step(j):
        cols = pl.ds(pl.multiple_of(j * unit, unit), unit)
        near, other = half_cols(b), half_cols(ob)
        lad[:, cols] = (
            dot(left[:, near], own_h[:, :, cols].reshape(rows, unit))
            + dot(left[:, other], far_h[:, :, cols].reshape(rows, unit))
            - dot(right[:, near], own_g[:, :, cols].reshape(rows, unit))
            - dot(right[:, other], far_g[:, :, cols].reshape(rows, unit))
        )

    each(columns // unit, ladder_step)

    def ph_scale(d):
        factor = ph_ref[...]
        left[strip(d), :] = (cross_g[slot(b, d), :].astype(jnp.float32) * factor).astype(jnp.bfloat16)
        right[strip(d), :] = (cross_h[slot(b, d), :].astype(jnp.float32) * factor).astype(jnp.bfloat16)

    ph_scale(c)

    def take(i):
        d = source(i)
        for t in range(2):
            piece_copy(t, d, d).wait_recv()
            relay(t, b, d).start()
        ph_scale(d)

    each(n - 1, take)

    def take_relay(d):
        for t in range(2):
            relay(t, ob, d).wait_recv()

    each(n, take_relay)

    for j in range(parts):
        cols = pl.ds(starts[j], widths[j])
        back[j][...] = (dot(left[...], cross_h[:, cols]) - dot(right[...], cross_g[:, cols])).astype(
            jnp.bfloat16
        )

        def give(i, j=j):
            back_copy(j, target(i), c).start()

        each(n - 1, give)
        back_local(j).start()

    first = b * rows
    for j in range(parts):

        def take_back(i, j=j):
            d = source(i)
            back_copy(j, d, d).wait_recv()

        each(n - 1, take_back)
        back_local(j).wait()
        cols = pl.ds(starts[j], widths[j])
        col_ids = starts[j] + lax.broadcasted_iota(jnp.int32, (1, widths[j]), 1)
        diag[:, cols] = jnp.zeros((1, widths[j]), jnp.float32)

        def fold(p, j=j, cols=cols, col_ids=col_ids):
            ids = row_ids + (first + p * piece)
            value = lad[strip(p), cols] + ret[j][partner_ref[p]].astype(jnp.float32) * coupling_ref[p]
            value = jnp.where((ids < length) & (col_ids < length), value, 0.0)
            out[strip(p), cols] = value.astype(jnp.bfloat16)
            diag[:, cols] += jnp.sum(jnp.where(ids == col_ids, value, 0.0), axis=0, keepdims=True)

        each(n, fold)
        out_copy(j).start()

    weighted = diag[:, half_cols(b)] * weight_ref[0]
    hits = lax.broadcasted_iota(jnp.int32, (orbits, rows), 0) == orbital_ref[...]
    part[...] = lax.dot_general(
        weighted,
        jnp.where(hits, 1.0, 0.0),
        (((1,), (1,)), ((), ())),
        precision=lax.Precision.HIGHEST,
        preferred_element_type=jnp.float32,
    )

    def total_send(i):
        total_copy(peer(i), me).start()

    each(count - 1, total_send)
    slots[me] = part[...]

    for t in range(2):
        twin_copy(t).wait_send()

    def drain(i):
        k = target(i)
        for t in range(2):
            piece_copy(t, k, c).wait_send()
        for j in range(parts):
            back_copy(j, k, c).wait_send()

    each(n - 1, drain)

    def drain_relay(d):
        for t in range(2):
            relay(t, b, d).wait_send()

    each(n, drain_relay)

    def total_take(i):
        other = peer(i)
        total_copy(other, me).wait_send()
        total_copy(other, other).wait_recv()

    each(count - 1, total_take)
    sum_ref[...] = jnp.sum(slots[...], axis=0) * scale
    for j in range(parts):
        out_copy(j).wait()


def on_device(
    generator,
    hamiltonian,
    pp_occupancy,
    ph_occupancy,
    lengths,
    partner,
    coupling,
    degeneracy,
    orbital,
):
    n = lax.axis_size("chan")
    m = lax.axis_size("blk")
    rows, columns = generator.shape[1:]
    widths = widths_of(columns)
    parts = len(widths)
    orbits = -(-NOB // 128) * 128
    anywhere = pl.BlockSpec(memory_space=pl.ANY)
    vmem = pl.BlockSpec(memory_space=pltpu.VMEM)
    smem = pl.BlockSpec(memory_space=pltpu.SMEM)
    dma = pltpu.SemaphoreType.DMA
    half = pltpu.VMEM((rows, columns), jnp.bfloat16)
    full = pltpu.VMEM((2 * rows, columns), jnp.bfloat16)
    cut = pltpu.VMEM((n, rows // n, columns), jnp.bfloat16)
    strips = [pltpu.VMEM((rows, w), jnp.bfloat16) for w in widths]
    cuts = [pltpu.VMEM((n, rows // n, w), jnp.bfloat16) for w in widths]
    scale = 1.0 / (8.0 * math.sqrt(n * columns / NOB))
    two_body, sums = pl.pallas_call(
        functools.partial(fused_kernel, n, m, widths, scale),
        out_shape=(
            jax.ShapeDtypeStruct((rows, columns), jnp.bfloat16),
            jax.ShapeDtypeStruct((1, orbits), jnp.float32),
        ),
        in_specs=[anywhere] * 2 + [vmem] * 2 + [smem] * 4 + [vmem],
        out_specs=(anywhere, vmem),
        scratch_shapes=[cut] * 4
        + [half] * 2
        + [full] * 2
        + [half] * 2
        + [
            pltpu.VMEM((rows, columns), jnp.float32),
            half,
            pltpu.VMEM((1, columns), jnp.float32),
            pltpu.VMEM((1, orbits), jnp.float32),
            pltpu.VMEM((n * m, 1, orbits), jnp.float32),
        ]
        + strips
        + cuts
        + [
            dma((2,)),
            dma((2,)),
            dma((2,)),
            dma((2, n)),
            dma((2, n)),
            dma((2, n)),
            dma((2, n)),
            dma((parts,)),
            dma((parts, n)),
            dma((parts, n)),
            dma((parts,)),
            dma((n * m,)),
            dma((n * m,)),
        ],
        compiler_params=pltpu.CompilerParams(
            collective_id=0, has_side_effects=True, vmem_limit_bytes=VMEM_LIMIT
        ),
        name="fused",
    )(
        generator.reshape(n, rows // n, columns),
        hamiltonian.reshape(n, rows // n, columns),
        pp_occupancy,
        ph_occupancy,
        partner[0],
        coupling[0],
        lengths,
        degeneracy,
        orbital,
    )
    return (two_body[None], sums[0, :NOB])


def solution(mesh):
    placed = (
        P("chan", "blk", None),
        P("chan", "blk", None),
        P("chan", None),
        P("chan", None),
        P("chan"),
        P("chan", None),
        P("chan", None),
        P("chan"),
        P("chan", "blk"),
    )
    n, m = mesh.shape["chan"], mesh.shape["blk"]

    def body(*args):
        rows, columns = args[0].shape[1:]
        tiled = m == 2 and n % 2 == 0 and rows % (16 * n) == 0 and columns % 256 == 0
        return (on_device if tiled else on_device_plain)(*args)

    return jax.shard_map(
        body,
        mesh=mesh,
        in_specs=placed,
        out_specs=(P("chan", "blk", None), P()),
        check_vma=False,
    )
```

profile of v0, /device:TPU:0, one launch (start us, length us, event | category | flops | bytes accessed | tf_op | source)
XLA Modules:
  0.0 185.4 jit_solution(14880716673611275223)
XLA Ops:
  1.9 179.7 %fused.1 = (bf16[768,1536]{1,0:T(8,128)(2,1)}, f32[1,256]{1,0:T(1,128)}) custom-call(bf16[16,48,1536]{2,1,0:T(8,128)(2,1)} %bitcast.8, bf16[16,48,1536]{2,1,0:T(8,128)(2,1)} %bitcast.9, f32[1,1536]{1,0:T(1,128)} %refs_2_.1, f32[1,1536]{1,0:T(1,128)} %refs_3_.1, s32[16]{0:T(128)} %bitcast.11, f32[16]{0:T(128)} %bitcast.12, s32[1]{0:T(128)S(6)} %copy.13.refs_6_, ...), custom_call_target="tpu_custom_call" | custom-call | tf_op jit(solution)/shard_map/fused/pallas_call | solution.py:468
  181.6 0.0 copy-start
  181.6 3.2 %copy.15 = bf16[1,768,1536]{2,1,0:T(8,128)(2,1)} copy(bf16[1,768,1536]{2,1,0:T(8,128)(2,1)} %bitcast.7) | data formatting | bytes 4718592
  184.8 0.0 copy-done
  184.8 0.6 copy.16
Async XLA Ops:
  181.6 3.2 %copy-start = (f32[1,256]{1,0:T(1,128)S(1)}, f32[1,256]{1,0:T(1,128)}, u32[]{:S(2)}) copy-start(f32[1,256]{1,0:T(1,128)} %get-tuple-element.5) | copy-start | bytes 3076
where the time goes:
time: 186 us; the launch traced here: 185 us
  Pallas kernels  180 us (97%)
  local copies, waits for them, and re-layouts  3.79 us (2%)
  between operations  1.94 us (1%)
    pallas_call x1, Pallas kernels, on_device(): pl.pallas_call(functools.partial(fused_kernel, n, m, widths, scale), out_...  180 us
    unnamed x4, local copies, waits for them, and re-layouts  3.79 us

commit v1 on v0

--- a/solution.py
+++ b/solution.py
@@ -163,7 +163,12 @@
     rows = n * piece
     orbits = part.shape[1]
     twin = (c, ob)
-    starts = [sum(widths[:j]) for j in range(parts)]
+    ends = [sum(widths[: j + 1]) for j in range(parts)]
+    starts = [
+        pl.multiple_of((1 - b) * (ends[j] - widths[j]) + b * (columns - ends[j]), 128)
+        for j in range(parts)
+    ]
+    middle = [end >= rows for end in ends].index(True)
     raw = ((gen_hbm, own_g, far_g), (ham_hbm, own_h, far_h))
     sent = ((send_g, cross_g), (send_h, cross_h))
     length = length_ref[0]
@@ -177,18 +182,24 @@
     def strip(d):
         return pl.ds(pl.multiple_of(d * piece, piece), piece)
 
-    def offset(i):
-        q = i // 2
-        turn = q % 2
-        far = n // 2 + (1 - 2 * turn) * ((q + 1) // 2)
-        near = (1 - turn) * (n - 1 - q // 2) + turn * ((q + 1) // 2)
-        return (1 - i % 2) * far + (i % 2) * near
+    level = n // 4
+    z, y, x = c // level, c % level // 2, c % 2
+
+    def chip(to, turn):
+        return to * level + (y + turn // 2) % (level // 2) * 2 + (x + turn) % 2
+
+    def pick(i, first, second, third):
+        q, r = i // level, i % level
+        own = q // 3
+        to = first * ((1 - q) * (2 - q) // 2) + second * (q * (2 - q)) + third * (q * (q - 1) // 2)
+        turn = r + b * (level - 1 - 2 * r)
+        return chip(to * (1 - own) + z * own, turn * (1 - own) + (r + 1) * own)
 
     def target(i):
-        return (c + offset(i)) % n
+        return pick(i, 1 + z % 2, 3 * (1 - z % 2), (z + 2) % 4)
 
     def source(i):
-        return (c + n - offset(i)) % n
+        return pick(i, z + 1 - 2 * (z % 2), 2 - z // 2, 3 * (1 - z // 2))
 
     def each(count, body, first=0):
         def step(i, carry):
@@ -298,16 +309,18 @@
 
     prepare_sent(0)
     pl.semaphore_wait(barrier, count - 1)
+    distant = n - level
 
     def prepare_and_send(i):
         prepare_sent(i)
         send(i - 1)
 
-    each(n - 1, prepare_and_send, 1)
+    each(distant, prepare_and_send, 1)
     prepare(c, [(cross_g, slot(b, c)), (cross_h, slot(b, c))])
-    send(n - 2)
+    send(distant - 1)
     for t in range(2):
         twin_copy(t).start()
+    each(n - 1, prepare_sent, distant)
 
     def pp_scale(i):
         factor = jnp.where(col_live, pp_ref[...], 0.0)
@@ -335,6 +348,7 @@
         )
 
     each(columns // unit, ladder_step)
+    each(n - 1, send, distant)
 
     def ph_scale(d):
         factor = ph_ref[...]
@@ -392,22 +406,23 @@
 
         each(n, fold)
         out_copy(j).start()
-
-    weighted = diag[:, half_cols(b)] * weight_ref[0]
-    hits = lax.broadcasted_iota(jnp.int32, (orbits, rows), 0) == orbital_ref[...]
-    part[...] = lax.dot_general(
-        weighted,
-        jnp.where(hits, 1.0, 0.0),
-        (((1,), (1,)), ((), ())),
-        precision=lax.Precision.HIGHEST,
-        preferred_element_type=jnp.float32,
-    )
-
-    def total_send(i):
-        total_copy(peer(i), me).start()
-
-    each(count - 1, total_send)
-    slots[me] = part[...]
+        if j != middle:
+            continue
+        weighted = diag[:, half_cols(b)] * weight_ref[0]
+        hits = lax.broadcasted_iota(jnp.int32, (orbits, rows), 0) == orbital_ref[...]
+        part[...] = lax.dot_general(
+            weighted,
+            jnp.where(hits, 1.0, 0.0),
+            (((1,), (1,)), ((), ())),
+            precision=lax.Precision.HIGHEST,
+            preferred_element_type=jnp.float32,
+        )
+
+        def total_send(i):
+            total_copy(peer(i), me).start()
+
+        each(count - 1, total_send)
+        slots[me] = part[...]
 
     for t in range(2):
         twin_copy(t).wait_send()
@@ -535,7 +550,7 @@
 
     def body(*args):
         rows, columns = args[0].shape[1:]
-        tiled = m == 2 and n % 2 == 0 and rows % (16 * n) == 0 and columns % 256 == 0
+        tiled = m == 2 and n % 8 == 0 and rows % (16 * n) == 0 and columns % 256 == 0
         return (on_device if tiled else on_device_plain)(*args)
 
     return jax.shard_map(

time: 186 us -> 174 us (0.935)
  Pallas kernels: 180 us -> 168 us
    pallas_call x1, Pallas kernels: 180 us -> 168 us  [on_device(): pl.pallas_call(functools.partial(fused_kernel, n, m, widths, scale), out_...]
where the time goes in v1:
time: 174 us
  Pallas kernels  168 us (97%)
  local copies, waits for them, and re-layouts  3.79 us (2%)
  between operations  1.94 us (1%)
    pallas_call x1, Pallas kernels, on_device(): pl.pallas_call(functools.partial(fused_kernel, n, m, widths, scale), out_...  168 us
    unnamed x4, local copies, waits for them, and re-layouts  3.79 us

profile of v1, /device:TPU:0, one launch (start us, length us, event | category | flops | bytes accessed | tf_op | source)
XLA Modules:
  0.0 174.2 jit_solution(13174645941113191536)
XLA Ops:
  1.9 168.5 %fused.1 = (bf16[768,1536]{1,0:T(8,128)(2,1)}, f32[1,256]{1,0:T(1,128)}) custom-call(bf16[16,48,1536]{2,1,0:T(8,128)(2,1)} %bitcast.8, bf16[16,48,1536]{2,1,0:T(8,128)(2,1)} %bitcast.9, f32[1,1536]{1,0:T(1,128)} %refs_2_.1, f32[1,1536]{1,0:T(1,128)} %refs_3_.1, s32[16]{0:T(128)} %bitcast.11, f32[16]{0:T(128)} %bitcast.12, s32[1]{0:T(128)S(6)} %copy.13.refs_6_, ...), custom_call_target="tpu_custom_call" | custom-call | tf_op jit(solution)/shard_map/fused/pallas_call | solution.py:483
  170.4 0.0 copy-start
  170.4 3.2 %copy.15 = bf16[1,768,1536]{2,1,0:T(8,128)(2,1)} copy(bf16[1,768,1536]{2,1,0:T(8,128)(2,1)} %bitcast.7) | data formatting | bytes 4718592
  173.7 0.0 copy-done
  173.7 0.6 copy.16
Async XLA Ops:
  170.4 3.2 %copy-start = (f32[1,256]{1,0:T(1,128)S(1)}, f32[1,256]{1,0:T(1,128)}, u32[]{:S(2)}) copy-start(f32[1,256]{1,0:T(1,128)} %get-tuple-element.5) | copy-start | bytes 3076

commit v2 on v1

--- a/solution.py
+++ b/solution.py
@@ -119,7 +119,7 @@
         length_ref,
         weight_ref,
         orbital_ref,
-        out_hbm,
+        out,
         sum_ref,
         own_g,
         own_h,
@@ -132,13 +132,12 @@
         left,
         right,
         lad,
-        out,
         diag,
         part,
         slots,
-    ) = refs[:26]
-    back = refs[26 : 26 + parts]
-    ret = refs[26 + parts : 26 + 2 * parts]
+    ) = refs[:25]
+    back = refs[25 : 25 + parts]
+    ret = refs[25 + parts : 25 + 2 * parts]
     (
         own_sem,
         x_send,
@@ -150,10 +149,9 @@
         l_sem,
         b_send,
         b_recv,
-        out_sem,
         t_send,
         t_recv,
-    ) = refs[26 + 2 * parts :]
+    ) = refs[25 + 2 * parts :]
     c = lax.axis_index("chan")
     b = lax.axis_index("blk")
     ob = 1 - b
@@ -198,6 +196,9 @@
     def target(i):
         return pick(i, 1 + z % 2, 3 * (1 - z % 2), (z + 2) % 4)
 
+    def giver(i):
+        return pick(i, 3 * (1 - z // 2), 2 - z // 2, z + 1 - 2 * (z % 2))
+
     def source(i):
         return pick(i, z + 1 - 2 * (z % 2), 2 - z // 2, 3 * (1 - z // 2))
 
@@ -254,10 +255,6 @@
     def back_local(j):
         return pltpu.make_async_copy(back[j].at[strip(c)], ret[j].at[c], l_sem.at[j])
 
-    def out_copy(j):
-        cols = pl.ds(starts[j], widths[j])
-        return pltpu.make_async_copy(out.at[:, cols], out_hbm.at[:, cols], out_sem.at[j])
-
     def peer(i):
         return (me + 1 + i) % count
 
@@ -276,10 +273,11 @@
     barrier = pltpu.get_barrier_semaphore()
 
     def greet(i):
-        to = peer(i)
-        pl.semaphore_signal(barrier, inc=1, device_id=(to // m, to % m), device_id_type=MESH)
-
-    each(count - 1, greet)
+        for core in range(m):
+            pl.semaphore_signal(barrier, inc=1, device_id=(giver(i), core), device_id_type=MESH)
+
+    each(n - 1, greet)
+    pl.semaphore_signal(barrier, inc=1, device_id=twin, device_id_type=MESH)
     for t in range(2):
         own_copy(t).wait()
 
@@ -307,17 +305,18 @@
         for t in range(2):
             piece_copy(t, k, c).start()
 
-    prepare_sent(0)
+    ahead = 2
+    each(ahead, prepare_sent)
     pl.semaphore_wait(barrier, count - 1)
     distant = n - level
 
-    def prepare_and_send(i):
-        prepare_sent(i)
-        send(i - 1)
-
-    each(distant, prepare_and_send, 1)
+    def send_and_prepare(i):
+        send(i)
+        prepare_sent(i + ahead)
+
+    each(distant - ahead, send_and_prepare)
+    each(distant, send, distant - ahead)
     prepare(c, [(cross_g, slot(b, c)), (cross_h, slot(b, c))])
-    send(distant - 1)
     for t in range(2):
         twin_copy(t).start()
     each(n - 1, prepare_sent, distant)
@@ -379,7 +378,7 @@
         )
 
         def give(i, j=j):
-            back_copy(j, target(i), c).start()
+            back_copy(j, giver(i), c).start()
 
         each(n - 1, give)
         back_local(j).start()
@@ -405,7 +404,6 @@
             diag[:, cols] += jnp.sum(jnp.where(ids == col_ids, value, 0.0), axis=0, keepdims=True)
 
         each(n, fold)
-        out_copy(j).start()
         if j != middle:
             continue
         weighted = diag[:, half_cols(b)] * weight_ref[0]
@@ -449,8 +447,6 @@
 
     each(count - 1, total_take)
     sum_ref[...] = jnp.sum(slots[...], axis=0) * scale
-    for j in range(parts):
-        out_copy(j).wait()
 
 
 def on_device(
@@ -483,18 +479,17 @@
     two_body, sums = pl.pallas_call(
         functools.partial(fused_kernel, n, m, widths, scale),
         out_shape=(
-            jax.ShapeDtypeStruct((rows, columns), jnp.bfloat16),
-            jax.ShapeDtypeStruct((1, orbits), jnp.float32),
+            pltpu.VMEM((rows, columns), jnp.bfloat16),
+            pltpu.VMEM((1, orbits), jnp.float32),
         ),
         in_specs=[anywhere] * 2 + [vmem] * 2 + [smem] * 4 + [vmem],
-        out_specs=(anywhere, vmem),
+        out_specs=(vmem, vmem),
         scratch_shapes=[cut] * 4
         + [half] * 2
         + [full] * 2
         + [half] * 2
         + [
             pltpu.VMEM((rows, columns), jnp.float32),
-            half,
             pltpu.VMEM((1, columns), jnp.float32),
             pltpu.VMEM((1, orbits), jnp.float32),
             pltpu.VMEM((n * m, 1, orbits), jnp.float32),
@@ -512,7 +507,6 @@
             dma((parts,)),
             dma((parts, n)),
             dma((parts, n)),
-            dma((parts,)),
             dma((n * m,)),
             dma((n * m,)),
         ],

time: 174 us -> 171 us (0.983)
  Pallas kernels: 168 us -> 166 us
  local copies, waits for them, and re-layouts: 3.79 us -> 1.97 us
    pallas_call x1, Pallas kernels: 168 us -> 166 us  [on_device(): pl.pallas_call(functools.partial(fused_kernel, n, m, widths, scale), out_...]
    unnamed x4 -> x2, local copies, waits for them, and re-layouts: 3.79 us -> 1.97 us
where the time goes in v2:
time: 171 us; the launch traced here: 170 us
  Pallas kernels  166 us (97%)
  local copies, waits for them, and re-layouts  1.97 us (1%)
  between operations  1.93 us (1%)
    pallas_call x1, Pallas kernels, on_device(): pl.pallas_call(functools.partial(fused_kernel, n, m, widths, scale), out_...  166 us

profile of v2, /device:TPU:0, one launch (start us, length us, event | category | flops | bytes accessed | tf_op | source)
XLA Modules:
  0.0 170.4 jit_solution(4335563479233931837)
XLA Ops:
  1.9 166.5 %fused.1 = (bf16[768,1536]{1,0:T(8,128)(2,1)S(1)}, f32[1,256]{1,0:T(1,128)S(1)}) custom-call(bf16[16,48,1536]{2,1,0:T(8,128)(2,1)} %bitcast.9, bf16[16,48,1536]{2,1,0:T(8,128)(2,1)} %bitcast.10, f32[1,1536]{1,0:T(1,128)} %refs_2_.1, f32[1,1536]{1,0:T(1,128)} %refs_3_.1, s32[16]{0:T(128)} %bitcast.11, f32[16]{0:T(128)} %bitcast.12, s32[1]{0:T(128)S(6)} %copy.14.refs_6_, ...), custom_call_target="tpu_custom_call" | custom-call | tf_op jit(solution)/shard_map/fused/pallas_call | solution.py:479
  168.4 1.4 copy.13
  169.8 0.6 copy.16

commit v3 on v2

--- a/solution.py
+++ b/solution.py
@@ -112,6 +112,15 @@
     (
         gen_hbm,
         ham_hbm,
+        pp_hbm,
+        ph_hbm,
+        partner_hbm,
+        coupling_hbm,
+        length_hbm,
+        weight_hbm,
+        orbital_hbm,
+        out,
+        sum_ref,
         pp_ref,
         ph_ref,
         partner_ref,
@@ -119,8 +128,6 @@
         length_ref,
         weight_ref,
         orbital_ref,
-        out,
-        sum_ref,
         own_g,
         own_h,
         far_g,
@@ -135,10 +142,11 @@
         diag,
         part,
         slots,
-    ) = refs[:25]
-    back = refs[25 : 25 + parts]
-    ret = refs[25 + parts : 25 + 2 * parts]
+    ) = refs[:32]
+    back = refs[32 : 32 + parts]
+    ret = refs[32 + parts : 32 + 2 * parts]
     (
+        small_sem,
         own_sem,
         x_send,
         x_recv,
@@ -151,7 +159,7 @@
         b_recv,
         t_send,
         t_recv,
-    ) = refs[25 + 2 * parts :]
+    ) = refs[32 + 2 * parts :]
     c = lax.axis_index("chan")
     b = lax.axis_index("blk")
     ob = 1 - b
@@ -169,7 +177,15 @@
     middle = [end >= rows for end in ends].index(True)
     raw = ((gen_hbm, own_g, far_g), (ham_hbm, own_h, far_h))
     sent = ((send_g, cross_g), (send_h, cross_h))
-    length = length_ref[0]
+    small = (
+        (pp_hbm, pp_ref),
+        (ph_hbm, ph_ref),
+        (partner_hbm, partner_ref),
+        (coupling_hbm, coupling_ref),
+        (length_hbm, length_ref),
+        (weight_hbm, weight_ref),
+        (orbital_hbm, orbital_ref),
+    )
 
     def half_cols(half):
         return pl.ds(pl.multiple_of(half * rows, 128), rows)
@@ -209,6 +225,9 @@
 
         lax.fori_loop(first, count, step, 0)
 
+    def small_copy(i):
+        return pltpu.make_async_copy(small[i][0], small[i][1], small_sem.at[i])
+
     def own_copy(t):
         return pltpu.make_async_copy(raw[t][0], raw[t][1], own_sem.at[t])
 
@@ -226,7 +245,7 @@
         return pltpu.make_async_remote_copy(
             src_ref=sent[t][0].at[strip(k)],
             dst_ref=sent[t][1].at[slot(b, d)],
-            send_sem=a_send.at[t, k],
+            send_sem=a_send.at[t],
             recv_sem=a_recv.at[t, d],
             device_id=(k, b),
             device_id_type=MESH,
@@ -236,8 +255,8 @@
         return pltpu.make_async_remote_copy(
             src_ref=sent[t][1].at[slot(half, d)],
             dst_ref=sent[t][1].at[slot(half, d)],
-            send_sem=r_send.at[t, d],
-            recv_sem=r_recv.at[t, d],
+            send_sem=r_send.at[t],
+            recv_sem=r_recv.at[t],
             device_id=twin,
             device_id_type=MESH,
         )
@@ -246,9 +265,42 @@
         return pltpu.make_async_remote_copy(
             src_ref=back[j].at[strip(k)],
             dst_ref=ret[j].at[d],
-            send_sem=b_send.at[j, k],
-            recv_sem=b_recv.at[j, d],
+            send_sem=b_send.at[j],
+            recv_sem=b_recv.at[j],
             device_id=(k, b),
+            device_id_type=MESH,
+        )
+
+    others = pl.ds(0, (n - 1) * piece)
+
+    def all_pieces(t):
+        return pltpu.make_async_remote_copy(
+            src_ref=sent[t][0].at[others],
+            dst_ref=sent[t][1].at[others],
+            send_sem=a_send.at[t],
+            recv_sem=r_recv.at[t],
+            device_id=twin,
+            device_id_type=MESH,
+        )
+
+    def all_relays(t):
+        where = pl.ds(pl.multiple_of(ob * rows, rows), rows)
+        return pltpu.make_async_remote_copy(
+            src_ref=sent[t][1].at[where],
+            dst_ref=sent[t][1].at[where],
+            send_sem=r_send.at[t],
+            recv_sem=r_recv.at[t],
+            device_id=twin,
+            device_id_type=MESH,
+        )
+
+    def all_back(j):
+        return pltpu.make_async_remote_copy(
+            src_ref=back[j].at[others],
+            dst_ref=ret[j].at[pl.ds(0, n - 1)],
+            send_sem=b_send.at[j],
+            recv_sem=b_recv.at[j],
+            device_id=twin,
             device_id_type=MESH,
         )
 
@@ -268,6 +320,8 @@
             device_id_type=MESH,
         )
 
+    for i in range(len(small)):
+        small_copy(i).start()
     for t in range(2):
         own_copy(t).start()
     barrier = pltpu.get_barrier_semaphore()
@@ -278,8 +332,11 @@
 
     each(n - 1, greet)
     pl.semaphore_signal(barrier, inc=1, device_id=twin, device_id_type=MESH)
+    for i in range(len(small)):
+        small_copy(i).wait()
     for t in range(2):
         own_copy(t).wait()
+    length = length_ref[...]
 
     col_live = lax.broadcasted_iota(jnp.int32, (1, columns), 1) < length
     row_ids = lax.broadcasted_iota(jnp.int32, (piece, 1), 0)
@@ -365,11 +422,8 @@
 
     each(n - 1, take)
 
-    def take_relay(d):
-        for t in range(2):
-            relay(t, ob, d).wait_recv()
-
-    each(n, take_relay)
+    for t in range(2):
+        all_relays(t).wait_recv()
 
     for j in range(parts):
         cols = pl.ds(starts[j], widths[j])
@@ -383,30 +437,42 @@
         each(n - 1, give)
         back_local(j).start()
 
+    for t in range(2):
+        twin_copy(t).wait_send()
+        all_pieces(t).wait_send()
+        all_relays(t).wait_send()
+
+    def total_take(i):
+        other = peer(i)
+        total_copy(other, me).wait_send()
+        total_copy(other, other).wait_recv()
+
     first = b * rows
     for j in range(parts):
-
-        def take_back(i, j=j):
-            d = source(i)
-            back_copy(j, d, d).wait_recv()
-
-        each(n - 1, take_back)
+        if j + 1 == parts:
+            each(count - 1, total_take)
+            sum_ref[...] = jnp.sum(slots[...], axis=0) * scale
+            for i in range(j):
+                all_back(i).wait_send()
+        all_back(j).wait_recv()
         back_local(j).wait()
         cols = pl.ds(starts[j], widths[j])
         col_ids = starts[j] + lax.broadcasted_iota(jnp.int32, (1, widths[j]), 1)
-        diag[:, cols] = jnp.zeros((1, widths[j]), jnp.float32)
+        if j <= middle:
+            diag[:, cols] = jnp.zeros((1, widths[j]), jnp.float32)
 
         def fold(p, j=j, cols=cols, col_ids=col_ids):
             ids = row_ids + (first + p * piece)
             value = lad[strip(p), cols] + ret[j][partner_ref[p]].astype(jnp.float32) * coupling_ref[p]
             value = jnp.where((ids < length) & (col_ids < length), value, 0.0)
             out[strip(p), cols] = value.astype(jnp.bfloat16)
-            diag[:, cols] += jnp.sum(jnp.where(ids == col_ids, value, 0.0), axis=0, keepdims=True)
+            if j <= middle:
+                diag[:, cols] += jnp.sum(jnp.where(ids == col_ids, value, 0.0), axis=0, keepdims=True)
 
         each(n, fold)
         if j != middle:
             continue
-        weighted = diag[:, half_cols(b)] * weight_ref[0]
+        weighted = diag[:, half_cols(b)] * weight_ref[...]
         hits = lax.broadcasted_iota(jnp.int32, (orbits, rows), 0) == orbital_ref[...]
         part[...] = lax.dot_general(
             weighted,
@@ -422,31 +488,7 @@
         each(count - 1, total_send)
         slots[me] = part[...]
 
-    for t in range(2):
-        twin_copy(t).wait_send()
-
-    def drain(i):
-        k = target(i)
-        for t in range(2):
-            piece_copy(t, k, c).wait_send()
-        for j in range(parts):
-            back_copy(j, k, c).wait_send()
-
-    each(n - 1, drain)
-
-    def drain_relay(d):
-        for t in range(2):
-            relay(t, b, d).wait_send()
-
-    each(n, drain_relay)
-
-    def total_take(i):
-        other = peer(i)
-        total_copy(other, me).wait_send()
-        total_copy(other, other).wait_recv()
-
-    each(count - 1, total_take)
-    sum_ref[...] = jnp.sum(slots[...], axis=0) * scale
+    all_back(parts - 1).wait_send()
 
 
 def on_device(
@@ -467,8 +509,8 @@
     parts = len(widths)
     orbits = -(-NOB // 128) * 128
     anywhere = pl.BlockSpec(memory_space=pl.ANY)
+    hbm = pl.BlockSpec(memory_space=pltpu.HBM)
     vmem = pl.BlockSpec(memory_space=pltpu.VMEM)
-    smem = pl.BlockSpec(memory_space=pltpu.SMEM)
     dma = pltpu.SemaphoreType.DMA
     half = pltpu.VMEM((rows, columns), jnp.bfloat16)
     full = pltpu.VMEM((2 * rows, columns), jnp.bfloat16)
@@ -482,9 +524,18 @@
             pltpu.VMEM((rows, columns), jnp.bfloat16),
             pltpu.VMEM((1, orbits), jnp.float32),
         ),
-        in_specs=[anywhere] * 2 + [vmem] * 2 + [smem] * 4 + [vmem],
+        in_specs=[anywhere] * 2 + [hbm] * 7,
         out_specs=(vmem, vmem),
-        scratch_shapes=[cut] * 4
+        scratch_shapes=[
+            pltpu.VMEM((1, columns), jnp.float32),
+            pltpu.VMEM((1, columns), jnp.float32),
+            pltpu.SMEM((n,), jnp.int32),
+            pltpu.SMEM((n,), jnp.float32),
+            pltpu.VMEM((1, 1), jnp.int32),
+            pltpu.VMEM((1, 1), jnp.float32),
+            pltpu.VMEM((1, rows), jnp.int32),
+        ]
+        + [cut] * 4
         + [half] * 2
         + [full] * 2
         + [half] * 2
@@ -497,16 +548,17 @@
         + strips
         + cuts
         + [
+            dma((7,)),
+            dma((2,)),
             dma((2,)),
             dma((2,)),
             dma((2,)),
             dma((2, n)),
-            dma((2, n)),
-            dma((2, n)),
-            dma((2, n)),
+            dma((2,)),
+            dma((2,)),
             dma((parts,)),
-            dma((parts, n)),
-            dma((parts, n)),
+            dma((parts,)),
+            dma((parts,)),
             dma((n * m,)),
             dma((n * m,)),
         ],
@@ -521,8 +573,8 @@
         ph_occupancy,
         partner[0],
         coupling[0],
-        lengths,
-        degeneracy,
+        lengths[None],
+        degeneracy[None],
         orbital,
     )
     return (two_body[None], sums[0, :NOB])

time: 171 us -> 169 us (0.988)
  no operation moved by 1% of the time
where the time goes in v3:
time: 169 us
  Pallas kernels  165 us (98%)
  local copies, waits for them, and re-layouts  1.97 us (1%)
  between operations  1.93 us (1%)
    pallas_call x1, Pallas kernels, on_device(): pl.pallas_call(functools.partial(fused_kernel, n, m, widths, scale), out_...  165 us

profile of v3, /device:TPU:0, one launch (start us, length us, event | category | flops | bytes accessed | tf_op | source)
XLA Modules:
  0.0 168.9 jit_solution(10789914267729415717)
XLA Ops:
  1.9 165.0 %fused.1 = (bf16[768,1536]{1,0:T(8,128)(2,1)S(1)}, f32[1,256]{1,0:T(1,128)S(1)}) custom-call(bf16[16,48,1536]{2,1,0:T(8,128)(2,1)} %bitcast.13, bf16[16,48,1536]{2,1,0:T(8,128)(2,1)} %bitcast.14, f32[1,1536]{1,0:T(1,128)} %refs_2_.1, f32[1,1536]{1,0:T(1,128)} %refs_3_.1, s32[16]{0:T(128)} %bitcast.15, f32[16]{0:T(128)} %bitcast.16, s32[1,1]{1,0:T(1,128)} %bitcast.9.refs_6_, ...), custom_call_target="tpu_custom_call" | custom-call | tf_op jit(solution)/shard_map/fused/pallas_call | solution.py:521
  167.0 1.4 copy.13
  168.4 0.6 copy.16

commit v4 on v3

--- a/solution.py
+++ b/solution.py
@@ -218,12 +218,12 @@
     def source(i):
         return pick(i, z + 1 - 2 * (z % 2), 2 - z // 2, 3 * (1 - z // 2))
 
-    def each(count, body, first=0):
+    def each(count, body, first=0, unroll=1):
         def step(i, carry):
             body(i)
             return carry
 
-        lax.fori_loop(first, count, step, 0)
+        lax.fori_loop(first, count, step, 0, unroll=unroll)
 
     def small_copy(i):
         return pltpu.make_async_copy(small[i][0], small[i][1], small_sem.at[i])
@@ -425,17 +425,21 @@
     for t in range(2):
         all_relays(t).wait_recv()
 
+    def give(j):
+        def step(i):
+            back_copy(j, giver(i), c).start()
+
+        each(n - 1, step)
+        back_local(j).start()
+
     for j in range(parts):
         cols = pl.ds(starts[j], widths[j])
         back[j][...] = (dot(left[...], cross_h[:, cols]) - dot(right[...], cross_g[:, cols])).astype(
             jnp.bfloat16
         )
 
-        def give(i, j=j):
-            back_copy(j, giver(i), c).start()
-
-        each(n - 1, give)
-        back_local(j).start()
+        if j <= middle + 1:
+            give(j)
 
     for t in range(2):
         twin_copy(t).wait_send()
@@ -469,7 +473,7 @@
             if j <= middle:
                 diag[:, cols] += jnp.sum(jnp.where(ids == col_ids, value, 0.0), axis=0, keepdims=True)
 
-        each(n, fold)
+        each(n, fold, unroll=4)
         if j != middle:
             continue
         weighted = diag[:, half_cols(b)] * weight_ref[...]
@@ -486,6 +490,8 @@
             total_copy(peer(i), me).start()
 
         each(count - 1, total_send)
+        for i in range(middle + 2, parts):
+            give(i)
         slots[me] = part[...]
 
     all_back(parts - 1).wait_send()

time: 169 us -> 167 us (0.988)
  Pallas kernels: 165 us -> 163 us
    pallas_call x1, Pallas kernels: 165 us -> 163 us  [on_device(): pl.pallas_call(functools.partial(fused_kernel, n, m, widths, scale), out_...]
where the time goes in v4:
time: 167 us
  Pallas kernels  163 us (98%)
  local copies, waits for them, and re-layouts  1.97 us (1%)
  between operations  1.93 us (1%)
    pallas_call x1, Pallas kernels, on_device(): pl.pallas_call(functools.partial(fused_kernel, n, m, widths, scale), out_...  163 us

profile of v4, /device:TPU:0, one launch (start us, length us, event | category | flops | bytes accessed | tf_op | source)
XLA Modules:
  0.0 166.9 jit_solution(15383123175001180196)
XLA Ops:
  1.9 163.0 %fused.1 = (bf16[768,1536]{1,0:T(8,128)(2,1)S(1)}, f32[1,256]{1,0:T(1,128)S(1)}) custom-call(bf16[16,48,1536]{2,1,0:T(8,128)(2,1)} %bitcast.13, bf16[16,48,1536]{2,1,0:T(8,128)(2,1)} %bitcast.14, f32[1,1536]{1,0:T(1,128)} %refs_2_.1, f32[1,1536]{1,0:T(1,128)} %refs_3_.1, s32[16]{0:T(128)} %bitcast.15, f32[16]{0:T(128)} %bitcast.16, s32[1,1]{1,0:T(1,128)} %bitcast.9.refs_6_, ...), custom_call_target="tpu_custom_call" | custom-call | tf_op jit(solution)/shard_map/fused/pallas_call | solution.py:527
  164.9 1.4 copy.13
  166.4 0.6 copy.16
